TPU v7x, 256 devices: a whole 4x4x8 slice. The times are simulated.
256 devices in a mesh: level: 4 (over y), gx: 8 (over z_lo, x), gy: 8 (over z_hi, core).
Axes of the slice: x: 4, y: 4, z: 8 (z_hi: 4, z_lo: 2; z = z_hi * 2 + z_lo), core: 2. Of those that a mesh axis runs over, the one named last changes fastest.
Arguments:
- state: float32 [5, 64, 128, 128], P(None, 'gx', 'gy'), may hold values from -0.75 to 5.3, as said below
Outputs:
- level_states: float32 [4, 5, 64, 128, 128], P('level', None, 'gx', 'gy')
Inputs may be any that keep to these rules, and one draw needn't show every extreme that they name: state[0] is a density from 1.5 to 3; state[1:4] are the density times velocity components, each velocity component of magnitude at most 0.25; state[4] is the total energy, a pressure from 1 to 2 divided by 0.4 plus the kinetic energy.
All inputs are finite; a program needn't handle non-finite values.
Results may differ from a plain program's by a relative error of at most 0.0001.
Values sent between devices are 32-bit elements; how exact they have to be, the bound alone decides.
A program may use at most 64 MiB of HBM per device.

v0:
```python
import jax
import jax.numpy as jnp
from jax import lax
from jax.experimental import pallas as pl
from jax.experimental.pallas import tpu as pltpu
from jax.sharding import PartitionSpec as P

DT = 0.1
A1 = (4.0 / 5.0, -1.0 / 5.0, 4.0 / 105.0, -1.0 / 280.0)
B0 = -205.0 / 72.0
B1 = (8.0 / 5.0, -1.0 / 5.0, 8.0 / 315.0, -1.0 / 560.0)
MU = 0.1

S, U01, U02, U03, U21, U31, U22, U13, U32, U23, U11, U12 = range(12)
SENT = 10
F0, TA1, TA2, TA3, TB1, TB2, TB3, TC1, TC2, TC3, TD1, TD2 = range(12)


def tendency(xe, yh):
    own = slice(4, 8)
    u = [jnp.concatenate([xe[i], yh[i]], axis=0) for i in range(5)]
    rho, m, e = u[0], u[1:4], u[4]
    inv = 1.0 / rho
    v = [mi * inv for mi in m]
    k = 0.5 * (v[0] * v[0] + v[1] * v[1] + v[2] * v[2])
    p = 0.4 * (e - rho * k)
    q = k + p * inv
    h = e + p
    diffused = [None, v[0], v[1], v[2], q]

    def flux(direction, part):
        along = part(v[direction])
        rows = [part(m[i]) * along + (part(p) if i == direction else 0.0) for i in range(3)]
        return [part(m[direction])] + rows + [part(h) * along]

    row = lax.broadcasted_iota(jnp.int32, (4, 8, 128), 1)
    ends_y = {}
    for w in (1, 2, 3, 4):
        ends_y[w] = (row < w, row >= 8 - w)

    def x_shifts(a, w):
        return a[4 + w : 8 + w], a[4 - w : 8 - w]

    def y_shifts(a, w):
        mine, other = a
        up = pltpu.roll(jnp.where(ends_y[w][0], other, mine), 8 - w, 1)
        down = pltpu.roll(jnp.where(ends_y[w][1], other, mine), w, 1)
        return up, down

    def z_shifts(a, w):
        return pltpu.roll(a, 128 - w, 2), pltpu.roll(a, w, 2)

    def xpart(a):
        return a[0:12]

    def ypart(a):
        return a[4:8], a[12:16]

    flux_x = flux(0, xpart)
    flux_ym = flux(1, lambda a: a[4:8])
    flux_yo = flux(1, lambda a: a[12:16])
    flux_z = flux(2, lambda a: a[4:8])
    out = []
    for c in range(5):
        total = None
        if diffused[c] is not None:
            total = (3.0 * MU * B0) * diffused[c][own]
        for shifts, f, part in (
            (x_shifts, flux_x[c], xpart),
            (y_shifts, (flux_ym[c], flux_yo[c]), ypart),
            (z_shifts, flux_z[c], lambda a: a[4:8]),
        ):
            for w in (1, 2, 3, 4):
                up, down = shifts(f, w)
                term = (-A1[w - 1]) * (up - down)
                total = term if total is None else total + term
                if diffused[c] is not None:
                    up, down = shifts(part(diffused[c]), w)
                    total = total + (MU * B1[w - 1]) * (up + down)
        out.append(total)
    return out


def kernel(nx, nzh, state, out, xe, ry, sy, yh, g, fin, load_sem, in_sem, send_sem, recv_sem, osend_sem, orecv_sem):
    y = lax.axis_index("level")
    gx = lax.axis_index("gx")
    gy = lax.axis_index("gy")
    zh, c = gy // 2, gy % 2
    pos = y + (zh % 2) * (3 - 2 * y)
    half, rows = pos // 2, pl.multiple_of((pos % 2) * 8, 8)
    nyi = 4 * nzh
    yi = zh * 4 + pos

    def at_y(index):
        zh2, pos2 = index // 4, index % 4
        return (pos2 + (zh2 % 2) * (3 - 2 * pos2), gx, zh2 * 2 + c)

    up_x = (y, (gx + c) % nx, zh * 2 + 1 - c)
    down_x = (y, (gx + nx - 1 + c) % nx, zh * 2 + 1 - c)
    up_y = at_y((yi + 1) % nyi)
    down_y = at_y((yi + nyi - 1) % nyi)
    partner = (y, gx, zh * 2 + 1 - c)
    outer_x = (y, (gx + nx + 2 * c - 1) % nx, zh * 2 + 1 - c)

    barrier = pltpu.get_barrier_semaphore()
    peers = [outer_x, up_y, down_y, partner]
    for d in (1, 2, 3):
        for core in (0, 1):
            peers.append(((y + d) % 4, gx, zh * 2 + core))
    for peer in peers:
        pl.semaphore_signal(barrier, inc=1, device_id=peer, device_id_type=pl.DeviceIdType.MESH)

    def piece(core):
        return state.at[:, pl.ds(4 * core, 4), pl.ds(rows, 8), :]

    own = xe.at[S, :, pl.ds(4, 4)]
    load = pltpu.make_async_copy(piece(c), own, load_sem)
    give = pltpu.make_async_remote_copy(
        src_ref=piece(1 - c),
        dst_ref=own,
        send_sem=osend_sem.at[4],
        recv_sem=in_sem,
        device_id=partner,
        device_id_type=pl.DeviceIdType.MESH,
    )

    @pl.when(c == half)
    def _():
        load.start()

    pl.semaphore_wait(barrier, len(peers))

    @pl.when(c == half)
    def _():
        give.start()
        load.wait()

    @pl.when(c != half)
    def _():
        give.wait_recv()

    def copies(slot):
        mine = xe.at[slot, :, pl.ds(4, 4)]
        ends = (
            (sy.at[slot, 1], ry.at[slot, 1], up_y),
            (sy.at[slot, 0], ry.at[slot, 0], down_y),
            (mine, xe.at[slot, :, pl.ds(0, 4)], up_x),
            (mine, xe.at[slot, :, pl.ds(8, 4)], down_x),
        )
        return [
            pltpu.make_async_remote_copy(
                src_ref=src,
                dst_ref=dst,
                send_sem=send_sem.at[slot, i],
                recv_sem=recv_sem.at[slot, i],
                device_id=device,
                device_id_type=pl.DeviceIdType.MESH,
            )
            for i, (src, dst, device) in enumerate(ends)
        ]

    def send(slot, value=None):
        for i in range(5):
            if value is None:
                a = xe[slot, i, 4:8]
            else:
                a = value[i]
                xe[slot, i, 4:8] = a
            sy[slot, 0, i] = a[:, 0:4]
            sy[slot, 1, i] = a[:, 4:8]
        for copy in copies(slot):
            copy.start()

    def receive(slot):
        for copy in copies(slot):
            copy.wait_recv()
        for i in range(5):
            yh[slot, i] = jnp.concatenate([ry[slot, 0, i], ry[slot, 1, i]], axis=1)

    def evaluate(slot, into):
        result = tendency([xe[slot, i] for i in range(5)], [yh[slot, i] for i in range(5)])
        for i in range(5):
            g[into, i] = result[i]

    def mix(terms):
        parts = []
        for i in range(5):
            total = None
            for kind, slot, factor in terms:
                a = xe[slot, i, 4:8] if kind == "u" else g[slot, i]
                a = a if factor == 1.0 else factor * a
                total = a if total is None else total + a
            parts.append(total)
        return parts

    def everywhere(slot, terms):
        for ref in (xe, yh):
            for i in range(5):
                total = None
                for source, factor in terms:
                    a = factor * ref[source, i]
                    total = a if total is None else total + a
                ref[slot, i] = total

    def place(level):
        return out.at[0, :, pl.ds(4 * c, 4), pl.ds(rows, 8), :]

    def final(level, src):
        piece_sem = orecv_sem.at[(pos % 2) * 2 + c]
        here = jnp.logical_and(y == level, c == half)
        away = pltpu.make_async_remote_copy(
            src_ref=src,
            dst_ref=place(level),
            send_sem=osend_sem.at[level],
            recv_sem=piece_sem,
            device_id=(level, gx, zh * 2 + half),
            device_id_type=pl.DeviceIdType.MESH,
        )
        local = pltpu.make_async_copy(src, place(level), piece_sem)

        @pl.when(here)
        def _():
            local.start()

        @pl.when(jnp.logical_not(here))
        def _():
            away.start()

        return here, away

    send(S)
    receive(S)
    evaluate(S, F0)
    send(U01, mix([("u", S, 1.0), ("g", F0, DT)]))
    receive(U01)
    evaluate(U01, TA1)
    send(U02, mix([("u", U01, 1.0), ("g", TA1, DT)]))
    receive(U02)
    evaluate(U02, TA2)
    send(U03, mix([("u", U02, 1.0), ("g", TA2, DT)]))
    everywhere(U11, [(S, 0.5), (U02, 0.5)])
    evaluate(U11, TB1)
    send(U21, mix([("u", S, 1.0), ("g", F0, 0.5 * DT), ("g", TB1, 0.5 * DT)]))
    finals = [final(0, xe.at[U03, :, pl.ds(4, 4)])]
    receive(U03)
    evaluate(U03, TA3)
    receive(U21)
    evaluate(U21, TC1)
    send(U31, mix([("u", S, 1.0), ("g", F0, 0.5 * DT), ("g", TC1, 0.5 * DT)]))
    everywhere(U12, [(S, -5 / 12), (U01, -9 / 12), (U02, -3 / 12), (U03, 5 / 12), (U21, 2.0)])
    evaluate(U12, TB2)
    send(
        U22,
        mix(
            [("u", U21, 1.0), ("g", TC1, DT), ("g", TB1, -4 / 12 * DT), ("g", TB2, 5 / 12 * DT), ("g", F0, -1 / 12 * DT)]
        ),
    )
    send(
        U13,
        mix(
            [("u", U12, 1.0), ("g", TB2, DT), ("g", TA2, -4 / 12 * DT), ("g", TA3, 5 / 12 * DT), ("g", TA1, -1 / 12 * DT)]
        ),
    )
    finals.append(final(1, xe.at[U13, :, pl.ds(4, 4)]))
    receive(U31)
    evaluate(U31, TD1)
    receive(U22)
    evaluate(U22, TC2)
    send(
        U32,
        mix(
            [("u", U31, 1.0), ("g", TD1, DT), ("g", TC1, -4 / 12 * DT), ("g", TC2, 5 / 12 * DT), ("g", F0, -1 / 12 * DT)]
        ),
    )
    receive(U13)
    evaluate(U13, TB3)
    send(
        U23,
        mix(
            [("u", U22, 1.0), ("g", TC2, DT), ("g", TB2, -4 / 12 * DT), ("g", TB3, 5 / 12 * DT), ("g", TB1, -1 / 12 * DT)]
        ),
    )
    finals.append(final(2, xe.at[U23, :, pl.ds(4, 4)]))
    receive(U32)
    evaluate(U32, TD2)
    receive(U23)
    evaluate(U23, TC3)
    last = mix(
        [("u", U32, 1.0), ("g", TD2, DT), ("g", TC2, -4 / 12 * DT), ("g", TC3, 5 / 12 * DT), ("g", TC1, -1 / 12 * DT)]
    )
    for i in range(5):
        fin[i] = last[i]
    finals.append(final(3, fin))

    for slot in range(SENT):
        for copy in copies(slot):
            copy.wait_send()
    for here, away in finals:

        @pl.when(jnp.logical_not(here))
        def _(away=away):
            away.wait_send()

    @pl.when(c == half)
    def _():
        give.wait_send()

    for i in range(4):
        pltpu.make_async_copy(fin, place(3), orecv_sem.at[i]).wait()


def solution(mesh):
    nx, nzh = mesh.shape["gx"], mesh.shape["gy"] // 2

    def body(state):
        f32 = jnp.float32
        return pl.pallas_call(
            lambda *refs: kernel(nx, nzh, *refs),
            out_shape=jax.ShapeDtypeStruct((1,) + state.shape, f32),
            in_specs=[pl.BlockSpec(memory_space=pl.ANY)],
            out_specs=pl.BlockSpec(memory_space=OUT_SPACE),
            scratch_shapes=[
                pltpu.VMEM((12, 5, 12, 8, 128), f32),
                pltpu.VMEM((SENT, 2, 5, 4, 4, 128), f32),
                pltpu.VMEM((SENT, 2, 5, 4, 4, 128), f32),
                pltpu.VMEM((12, 5, 4, 8, 128), f32),
                pltpu.VMEM((12, 5, 4, 8, 128), f32),
                pltpu.VMEM((5, 4, 8, 128), f32),
                pltpu.SemaphoreType.DMA,
                pltpu.SemaphoreType.DMA,
                pltpu.SemaphoreType.DMA((SENT, 4)),
                pltpu.SemaphoreType.DMA((SENT, 4)),
                pltpu.SemaphoreType.DMA((5,)),
                pltpu.SemaphoreType.DMA((4,)),
            ],
            compiler_params=pltpu.CompilerParams(collective_id=0, has_side_effects=True),
            name="window",
        )(state)

    return jax.shard_map(
        body,
        mesh=mesh,
        in_specs=(P(None, "gx", "gy", None),),
        out_specs=P("level", None, "gx", "gy", None),
        check_vma=False,
    )


OUT_SPACE = pltpu.VMEM
```

profile of v0, /device:TPU:24, one launch (start us, length us, event | category | flops | bytes accessed | tf_op | source)
XLA Modules:
  0.0 50.3 jit_solution(18224166334490010437)
XLA Ops:
  0.0 48.6 %window.1 = f32[1,5,8,16,128]{4,3,2,1,0:T(8,128)} custom-call(f32[5,8,16,128]{3,2,1,0:T(8,128)} %refs_0_.1), custom_call_target="tpu_custom_call" | custom-call | tf_op jit(solution)/shard_map/window/pallas_call | solution.py:317
  48.6 1.7 %copy.3 = f32[1,5,8,16,128]{4,3,2,1,0:T(8,128)} copy(f32[1,5,8,16,128]{4,3,2,1,0:T(8,128)} %window.1) | data formatting | bytes 655360
where the time goes:
time: 50.4 us; the launch traced here: 50.3 us
  Pallas kernels  48.6 us (96%)
  local copies, waits for them, and re-layouts  1.72 us (3%)
    pallas_call x1, Pallas kernels, body(): pl.pallas_call(lambda *refs: kernel(nx, nzh, *refs), out_shape=jax.ShapeD...  48.6 us
    unnamed x1, local copies, waits for them, and re-layouts  1.72 us

commit v1 on v0

v1 whole, which is shorter than its diff:
```python
import jax
import jax.numpy as jnp
from jax import lax
from jax.experimental import pallas as pl
from jax.experimental.pallas import tpu as pltpu
from jax.sharding import PartitionSpec as P

DT = 0.1
A1 = (4.0 / 5.0, -1.0 / 5.0, 4.0 / 105.0, -1.0 / 280.0)
B0 = -205.0 / 72.0
B1 = (8.0 / 5.0, -1.0 / 5.0, 8.0 / 315.0, -1.0 / 560.0)
MU = 0.1

S, U01, U02, U03, U21, U31, U22, U13, U32, U23, U11, U12 = range(12)
SENT = 10
F0, TA1, TA2, TA3, TB1, TB2, TB3, TC1, TC2, TC3, TD1, TD2 = range(12)


def primitives(u):
    rho, m, e = u[0], u[1:4], u[4]
    inv = 1.0 / rho
    v = [mi * inv for mi in m]
    k = 0.5 * (v[0] * v[0] + v[1] * v[1] + v[2] * v[2])
    p = 0.4 * (e - rho * k)
    return m, v, p, e + p, k + p * inv


def flux(parts, d):
    m, v, p, h, _ = parts
    return [m[d]] + [m[i] * v[d] + p if i == d else m[i] * v[d] for i in range(3)] + [h * v[d]]


def diffused(parts):
    return [None, *parts[1], parts[4]]


def along(total, f, w, shifts):
    for n in (1, 2, 3, 4):
        up, down = shifts(f, n)
        term = (-A1[n - 1]) * (up - down)
        total = term if total is None else total + term
        if w is not None:
            up, down = shifts(w, n)
            total = total + (MU * B1[n - 1]) * (up + down)
    return total


def inner(u):
    parts = primitives(u)
    out = []
    for f, w in zip(flux(parts, 2), diffused(parts)):
        total = None if w is None else (3.0 * MU * B0) * w
        out.append(along(total, f, w, lambda a, n: (pltpu.roll(a, 128 - n, 2), pltpu.roll(a, n, 2))))
    return parts, out


def outer(state, low, high, ends):
    parts, out = state
    row = lax.broadcasted_iota(jnp.int32, (4, 8, 128), 1)
    before, after, edge = primitives(low), primitives(high), primitives(ends)

    def join(a, b, c):
        return None if b is None else jnp.concatenate([a, b, c], axis=0)

    fx = [join(*t) for t in zip(flux(before, 0), flux(parts, 0), flux(after, 0))]
    wx = [join(*t) for t in zip(diffused(before), diffused(parts), diffused(after))]
    out = [along(t, f, w, lambda a, n: (a[4 + n : 8 + n], a[4 - n : 8 - n])) for t, f, w in zip(out, fx, wx)]

    def y_shifts(a, n):
        mine, other = a
        up = pltpu.roll(jnp.where(row < n, other, mine), 8 - n, 1)
        down = pltpu.roll(jnp.where(row >= 8 - n, other, mine), n, 1)
        return up, down

    fy = zip(flux(parts, 1), flux(edge, 1))
    wy = [None if a is None else (a, b) for a, b in zip(diffused(parts), diffused(edge))]
    return [along(t, f, w, y_shifts) for t, f, w in zip(out, fy, wy)]


def kernel(nxp, nzh, state, out, xe, ry, sy, yh, g, fin, in_sem, send_sem, recv_sem, osend_sem, orecv_sem):
    y = lax.axis_index("level")
    gx = lax.axis_index("gx")
    gy = lax.axis_index("gy")
    h, c = gy // 2, gy % 2
    x, lo = gx % nxp, gx // nxp
    q = y // 2
    back = ((y + 1) // 2 + 1) % 2
    mine_x = back * nxp + x
    pos = q + lo * (3 - 2 * q)
    rows = pl.multiple_of((pos % 2) * 8, 8)
    nyi = 4 * nzh

    def owner(column, index, core):
        h2, pos2 = index // 4, index % 4
        lo2 = pos2 // 2
        q2 = pos2 + lo2 * (3 - 2 * pos2)
        return (1 + q2 + (column // nxp) * (2 * q2 - 1), lo2 * nxp + column % nxp, h2 * 2 + core)

    yi = h * 4 + pos
    nx = 2 * nxp
    up_x = owner((mine_x + c) % nx, yi, 1 - c)
    down_x = owner((mine_x + nx - 1 + c) % nx, yi, 1 - c)
    up_y = owner(mine_x, (yi + 1) % nyi, c)
    down_y = owner(mine_x, (yi + nyi - 1) % nyi, c)
    outer_x = owner((mine_x + nx + 2 * c - 1) % nx, yi, 1 - c)

    barrier = pltpu.get_barrier_semaphore()
    peers = [outer_x, up_y, down_y]
    for d in range(16):
        if d:
            peers.append(((y + d // 4) % 4, ((lo + d // 2 % 2) % 2) * nxp + x, h * 2 + (c + d) % 2))
    for peer in peers:
        pl.semaphore_signal(barrier, inc=1, device_id=peer, device_id_type=pl.DeviceIdType.MESH)

    own = xe.at[S, :, pl.ds(4, 4)]
    give_pos = q + c * (3 - 2 * q)
    holder = lo == back
    gives = []
    for core in (0, 1):
        src = state.at[:, pl.ds(4 * core, 4), pl.ds(pl.multiple_of((give_pos % 2) * 8, 8), 8), :]
        away = pltpu.make_async_remote_copy(
            src_ref=src,
            dst_ref=own,
            send_sem=osend_sem.at[4 + core],
            recv_sem=in_sem,
            device_id=(y, c * nxp + x, h * 2 + core),
            device_id_type=pl.DeviceIdType.MESH,
        )
        here = jnp.logical_and(c == lo, c == core)
        gives.append((here, away, pltpu.make_async_copy(src, own, in_sem)))

    pl.semaphore_wait(barrier, len(peers))

    @pl.when(holder)
    def _():
        for here, away, local in gives:
            pl.when(here)(local.start)
            pl.when(jnp.logical_not(here))(away.start)

    gives[0][2].wait()

    def copies(slot):
        mine = xe.at[slot, :, pl.ds(4, 4)]
        ends = (
            (mine, xe.at[slot, :, pl.ds(0, 4)], up_x),
            (mine, xe.at[slot, :, pl.ds(8, 4)], down_x),
            (sy.at[slot, 1], ry.at[slot, 1], up_y),
            (sy.at[slot, 0], ry.at[slot, 0], down_y),
        )
        return [
            pltpu.make_async_remote_copy(
                src_ref=src,
                dst_ref=dst,
                send_sem=send_sem.at[slot, i],
                recv_sem=recv_sem.at[slot, i],
                device_id=device,
                device_id_type=pl.DeviceIdType.MESH,
            )
            for i, (src, dst, device) in enumerate(ends)
        ]

    def send(slot, value=None):
        along = copies(slot)
        if value is None:
            value = [xe[slot, i, 4:8] for i in range(5)]
        else:
            for i in range(5):
                xe[slot, i, 4:8] = value[i]
        for copy in along[:2]:
            copy.start()
        for i in range(5):
            sy[slot, 0, i] = value[i][:, 0:4]
            sy[slot, 1, i] = value[i][:, 4:8]
        for copy in along[2:]:
            copy.start()

    def receive(slot):
        for copy in copies(slot):
            copy.wait_recv()
        for i in range(5):
            yh[slot, i] = jnp.concatenate([ry[slot, 0, i], ry[slot, 1, i]], axis=1)

    def begin(slot):
        return inner([xe[slot, i, 4:8] for i in range(5)])

    def evaluate(slot, into, begun):
        result = outer(begun, *([ref[slot, i, part] for i in range(5)] for ref, part in ((xe, slice(0, 4)), (xe, slice(8, 12)), (yh, slice(0, 4)))))
        for i in range(5):
            g[into, i] = result[i]

    def mix(terms):
        parts = []
        for i in range(5):
            total = None
            for kind, slot, factor in terms:
                a = xe[slot, i, 4:8] if kind == "u" else g[slot, i]
                a = a if factor == 1.0 else factor * a
                total = a if total is None else total + a
            parts.append(total)
        return parts

    def everywhere(slot, terms):
        for ref in (xe, yh):
            for i in range(5):
                total = None
                for source, factor in terms:
                    a = factor * ref[source, i]
                    total = a if total is None else total + a
                ref[slot, i] = total

    def place(level):
        return out.at[0, :, pl.ds(4 * c, 4), pl.ds(rows, 8), :]

    def final(level, src):
        piece_sem = orecv_sem.at[(pos % 2) * 2 + c]
        here = jnp.logical_and(jnp.logical_and(y == level, c == lo), lo == back)
        away = pltpu.make_async_remote_copy(
            src_ref=src,
            dst_ref=place(level),
            send_sem=osend_sem.at[level],
            recv_sem=piece_sem,
            device_id=(level, mine_x, h * 2 + lo),
            device_id_type=pl.DeviceIdType.MESH,
        )
        local = pltpu.make_async_copy(src, place(level), piece_sem)

        @pl.when(here)
        def _():
            local.start()

        @pl.when(jnp.logical_not(here))
        def _():
            away.start()

        return here, away

    send(S)
    begun = begin(S)
    receive(S)
    evaluate(S, F0, begun)
    send(U01, mix([("u", S, 1.0), ("g", F0, DT)]))
    begun = begin(U01)
    receive(U01)
    evaluate(U01, TA1, begun)
    send(U02, mix([("u", U01, 1.0), ("g", TA1, DT)]))
    begun = begin(U02)
    receive(U02)
    evaluate(U02, TA2, begun)
    send(U03, mix([("u", U02, 1.0), ("g", TA2, DT)]))
    everywhere(U11, [(S, 0.5), (U02, 0.5)])
    evaluate(U11, TB1, begin(U11))
    send(U21, mix([("u", S, 1.0), ("g", F0, 0.5 * DT), ("g", TB1, 0.5 * DT)]))
    finals = [final(0, xe.at[U03, :, pl.ds(4, 4)])]
    begun = begin(U03), begin(U21)
    receive(U03)
    evaluate(U03, TA3, begun[0])
    receive(U21)
    evaluate(U21, TC1, begun[1])
    send(U31, mix([("u", S, 1.0), ("g", F0, 0.5 * DT), ("g", TC1, 0.5 * DT)]))
    everywhere(U12, [(S, -5 / 12), (U01, -9 / 12), (U02, -3 / 12), (U03, 5 / 12), (U21, 2.0)])
    evaluate(U12, TB2, begin(U12))
    send(
        U22,
        mix(
            [("u", U21, 1.0), ("g", TC1, DT), ("g", TB1, -4 / 12 * DT), ("g", TB2, 5 / 12 * DT), ("g", F0, -1 / 12 * DT)]
        ),
    )
    send(
        U13,
        mix(
            [("u", U12, 1.0), ("g", TB2, DT), ("g", TA2, -4 / 12 * DT), ("g", TA3, 5 / 12 * DT), ("g", TA1, -1 / 12 * DT)]
        ),
    )
    finals.append(final(1, xe.at[U13, :, pl.ds(4, 4)]))
    begun = begin(U31), begin(U22), begin(U13)
    receive(U31)
    evaluate(U31, TD1, begun[0])
    receive(U22)
    evaluate(U22, TC2, begun[1])
    send(
        U32,
        mix(
            [("u", U31, 1.0), ("g", TD1, DT), ("g", TC1, -4 / 12 * DT), ("g", TC2, 5 / 12 * DT), ("g", F0, -1 / 12 * DT)]
        ),
    )
    receive(U13)
    evaluate(U13, TB3, begun[2])
    send(
        U23,
        mix(
            [("u", U22, 1.0), ("g", TC2, DT), ("g", TB2, -4 / 12 * DT), ("g", TB3, 5 / 12 * DT), ("g", TB1, -1 / 12 * DT)]
        ),
    )
    finals.append(final(2, xe.at[U23, :, pl.ds(4, 4)]))
    begun = begin(U32), begin(U23)
    receive(U32)
    evaluate(U32, TD2, begun[0])
    receive(U23)
    evaluate(U23, TC3, begun[1])
    last = mix(
        [("u", U32, 1.0), ("g", TD2, DT), ("g", TC2, -4 / 12 * DT), ("g", TC3, 5 / 12 * DT), ("g", TC1, -1 / 12 * DT)]
    )
    for i in range(5):
        fin[i] = last[i]
    finals.append(final(3, fin))

    for slot in range(SENT):
        for copy in copies(slot):
            copy.wait_send()
    for here, away in finals:

        @pl.when(jnp.logical_not(here))
        def _(away=away):
            away.wait_send()

    @pl.when(holder)
    def _():
        for here, away, _ in gives:
            pl.when(jnp.logical_not(here))(away.wait_send)

    for i in range(4):
        pltpu.make_async_copy(fin, place(3), orecv_sem.at[i]).wait()


def solution(mesh):
    nxp, nzh = mesh.shape["gx"] // 2, mesh.shape["gy"] // 2

    def body(state):
        f32 = jnp.float32
        return pl.pallas_call(
            lambda *refs: kernel(nxp, nzh, *refs),
            out_shape=jax.ShapeDtypeStruct((1,) + state.shape, f32),
            in_specs=[pl.BlockSpec(memory_space=pltpu.HBM)],
            out_specs=pl.BlockSpec(memory_space=OUT_SPACE),
            scratch_shapes=[
                pltpu.VMEM((12, 5, 12, 8, 128), f32),
                pltpu.VMEM((SENT, 2, 5, 4, 4, 128), f32),
                pltpu.VMEM((SENT, 2, 5, 4, 4, 128), f32),
                pltpu.VMEM((12, 5, 4, 8, 128), f32),
                pltpu.VMEM((12, 5, 4, 8, 128), f32),
                pltpu.VMEM((5, 4, 8, 128), f32),
                pltpu.SemaphoreType.DMA,
                pltpu.SemaphoreType.DMA((SENT, 4)),
                pltpu.SemaphoreType.DMA((SENT, 4)),
                pltpu.SemaphoreType.DMA((6,)),
                pltpu.SemaphoreType.DMA((4,)),
            ],
            compiler_params=pltpu.CompilerParams(collective_id=0, vmem_limit_bytes=24 * 2**20, has_side_effects=True),
            name="window",
        )(state)

    return jax.shard_map(
        body,
        mesh=mesh,
        in_specs=(P(None, "gx", "gy", None),),
        out_specs=P("level", None, "gx", "gy", None),
        check_vma=False,
    )


OUT_SPACE = pl.ANY
```

time: 50.4 us -> 47.1 us (0.935)
  Pallas kernels: 48.6 us -> 45.3 us
    pallas_call x1, Pallas kernels: 48.6 us -> 45.3 us  [body(): pl.pallas_call(lambda *refs: kernel(nxp, nzh, *refs), out_shape=jax.Shape...]
    unnamed x1 -> x3, local copies, waits for them, and re-layouts: 1.72 us -> 1.7 us
where the time goes in v1:
time: 47.1 us; the launch traced here: 47 us
  Pallas kernels  45.3 us (96%)
  local copies, waits for them, and re-layouts  1.7 us (4%)
    pallas_call x1, Pallas kernels, body(): pl.pallas_call(lambda *refs: kernel(nxp, nzh, *refs), out_shape=jax.Shape...  45.3 us
    unnamed x3, local copies, waits for them, and re-layouts  1.7 us

profile of v1, /device:TPU:24, one launch (start us, length us, event | category | flops | bytes accessed | tf_op | source)
XLA Modules:
  0.0 47.0 jit_solution(10633148872231768193)
XLA Ops:
  0.0 0.0 copy-start
  0.0 1.0 %copy-done = f32[5,8,16,128]{3,2,1,0:T(8,128)S(1)} copy-done((f32[5,8,16,128]{3,2,1,0:T(8,128)S(1)}, f32[5,8,16,128]{3,2,1,0:T(8,128)}, u32[]{:S(2)}) %copy-start) | copy-done | bytes 327704
  1.0 45.3 %window.1 = f32[1,5,8,16,128]{4,3,2,1,0:T(8,128)S(1)} custom-call(f32[5,8,16,128]{3,2,1,0:T(8,128)S(1)} %copy-done), custom_call_target="tpu_custom_call" | custom-call | tf_op jit(solution)/shard_map/window/pallas_call | solution.py:330
  46.3 0.7 %copy.3 = f32[1,5,8,16,128]{4,3,2,1,0:T(8,128)} copy(f32[1,5,8,16,128]{4,3,2,1,0:T(8,128)S(1)} %window.1) | data formatting | bytes 655360
Async XLA Ops:
  0.0 1.0 %copy-start = (f32[5,8,16,128]{3,2,1,0:T(8,128)S(1)}, f32[5,8,16,128]{3,2,1,0:T(8,128)}, u32[]{:S(2)}) copy-start(f32[5,8,16,128]{3,2,1,0:T(8,128)} %refs_0_.1) | copy-start | bytes 983044

commit v2 on v1

--- a/solution.py
+++ b/solution.py
@@ -188,10 +188,10 @@
         for i in range(5):
             g[into, i] = result[i]
 
-    def mix(terms):
+    def mix(*terms, base=None):
         parts = []
         for i in range(5):
-            total = None
+            total = None if base is None else base[i]
             for kind, slot, factor in terms:
                 a = xe[slot, i, 4:8] if kind == "u" else g[slot, i]
                 a = a if factor == 1.0 else factor * a
@@ -199,14 +199,18 @@
             parts.append(total)
         return parts
 
-    def everywhere(slot, terms):
-        for ref in (xe, yh):
+    inside = ((xe, slice(4, 8)),)
+    around = ((xe, slice(0, 4)), (xe, slice(8, 12)), (yh, slice(0, 4)))
+
+    def combine(slot, terms, where):
+        for ref, part in where:
             for i in range(5):
                 total = None
                 for source, factor in terms:
-                    a = factor * ref[source, i]
+                    a = ref[source, i, part]
+                    a = a if factor == 1.0 else factor * a
                     total = a if total is None else total + a
-                ref[slot, i] = total
+                ref[slot, i, part] = total
 
     def place(level):
         return out.at[0, :, pl.ds(4 * c, 4), pl.ds(rows, 8), :]
@@ -238,68 +242,64 @@
     begun = begin(S)
     receive(S)
     evaluate(S, F0, begun)
-    send(U01, mix([("u", S, 1.0), ("g", F0, DT)]))
+    send(U01, mix(("u", S, 1.0), ("g", F0, DT)))
     begun = begin(U01)
     receive(U01)
     evaluate(U01, TA1, begun)
-    send(U02, mix([("u", U01, 1.0), ("g", TA1, DT)]))
-    begun = begin(U02)
+    send(U02, mix(("u", U01, 1.0), ("g", TA1, DT)))
+    halves = ((S, 0.5), (U02, 0.5))
+    combine(U11, halves, inside)
+    begun = begin(U02), begin(U11)
+    half_way = mix(("u", S, 1.0), ("g", F0, 0.5 * DT))
     receive(U02)
-    evaluate(U02, TA2, begun)
-    send(U03, mix([("u", U02, 1.0), ("g", TA2, DT)]))
-    everywhere(U11, [(S, 0.5), (U02, 0.5)])
-    evaluate(U11, TB1, begin(U11))
-    send(U21, mix([("u", S, 1.0), ("g", F0, 0.5 * DT), ("g", TB1, 0.5 * DT)]))
+    evaluate(U02, TA2, begun[0])
+    send(U03, mix(("u", U02, 1.0), ("g", TA2, DT)))
+    combine(U11, halves, around)
+    evaluate(U11, TB1, begun[1])
+    send(U21, mix(("g", TB1, 0.5 * DT), base=half_way))
     finals = [final(0, xe.at[U03, :, pl.ds(4, 4)])]
-    begun = begin(U03), begin(U21)
+    old = ((S, -5 / 12), (U01, -9 / 12), (U02, -3 / 12))
+    new = ((U12, 1.0), (U03, 5 / 12), (U21, 2.0))
+    combine(U12, old, inside + around)
+    combine(U12, new, inside)
+    begun = begin(U03), begin(U21), begin(U12)
+    half_way = mix(("u", S, 1.0), ("g", F0, 0.5 * DT))
+    base22 = mix(("u", U21, 1.0), ("g", TB1, -4 / 12 * DT), ("g", F0, -1 / 12 * DT))
+    base13 = mix(("u", U12, 1.0), ("g", TA2, -4 / 12 * DT), ("g", TA1, -1 / 12 * DT))
     receive(U03)
     evaluate(U03, TA3, begun[0])
+    base13 = mix(("g", TA3, 5 / 12 * DT), base=base13)
     receive(U21)
     evaluate(U21, TC1, begun[1])
-    send(U31, mix([("u", S, 1.0), ("g", F0, 0.5 * DT), ("g", TC1, 0.5 * DT)]))
-    everywhere(U12, [(S, -5 / 12), (U01, -9 / 12), (U02, -3 / 12), (U03, 5 / 12), (U21, 2.0)])
-    evaluate(U12, TB2, begin(U12))
-    send(
-        U22,
-        mix(
-            [("u", U21, 1.0), ("g", TC1, DT), ("g", TB1, -4 / 12 * DT), ("g", TB2, 5 / 12 * DT), ("g", F0, -1 / 12 * DT)]
-        ),
-    )
-    send(
-        U13,
-        mix(
-            [("u", U12, 1.0), ("g", TB2, DT), ("g", TA2, -4 / 12 * DT), ("g", TA3, 5 / 12 * DT), ("g", TA1, -1 / 12 * DT)]
-        ),
-    )
+    send(U31, mix(("g", TC1, 0.5 * DT), base=half_way))
+    combine(U12, new, around)
+    base22 = mix(("g", TC1, DT), base=base22)
+    evaluate(U12, TB2, begun[2])
+    send(U22, mix(("g", TB2, 5 / 12 * DT), base=base22))
+    send(U13, mix(("g", TB2, DT), base=base13))
     finals.append(final(1, xe.at[U13, :, pl.ds(4, 4)]))
     begun = begin(U31), begin(U22), begin(U13)
+    base32 = mix(("u", U31, 1.0), ("g", TC1, -4 / 12 * DT), ("g", F0, -1 / 12 * DT))
+    base23 = mix(("u", U22, 1.0), ("g", TB2, -4 / 12 * DT), ("g", TB1, -1 / 12 * DT))
     receive(U31)
     evaluate(U31, TD1, begun[0])
+    base32 = mix(("g", TD1, DT), base=base32)
     receive(U22)
     evaluate(U22, TC2, begun[1])
-    send(
-        U32,
-        mix(
-            [("u", U31, 1.0), ("g", TD1, DT), ("g", TC1, -4 / 12 * DT), ("g", TC2, 5 / 12 * DT), ("g", F0, -1 / 12 * DT)]
-        ),
-    )
+    send(U32, mix(("g", TC2, 5 / 12 * DT), base=base32))
+    base23 = mix(("g", TC2, DT), base=base23)
     receive(U13)
     evaluate(U13, TB3, begun[2])
-    send(
-        U23,
-        mix(
-            [("u", U22, 1.0), ("g", TC2, DT), ("g", TB2, -4 / 12 * DT), ("g", TB3, 5 / 12 * DT), ("g", TB1, -1 / 12 * DT)]
-        ),
-    )
+    send(U23, mix(("g", TB3, 5 / 12 * DT), base=base23))
     finals.append(final(2, xe.at[U23, :, pl.ds(4, 4)]))
     begun = begin(U32), begin(U23)
+    base33 = mix(("u", U32, 1.0), ("g", TC2, -4 / 12 * DT), ("g", TC1, -1 / 12 * DT))
     receive(U32)
     evaluate(U32, TD2, begun[0])
+    base33 = mix(("g", TD2, DT), base=base33)
     receive(U23)
     evaluate(U23, TC3, begun[1])
-    last = mix(
-        [("u", U32, 1.0), ("g", TD2, DT), ("g", TC2, -4 / 12 * DT), ("g", TC3, 5 / 12 * DT), ("g", TC1, -1 / 12 * DT)]
-    )
+    last = mix(("g", TC3, 5 / 12 * DT), base=base33)
     for i in range(5):
         fin[i] = last[i]
     finals.append(final(3, fin))
@@ -347,7 +347,7 @@
             ],
             compiler_params=pltpu.CompilerParams(collective_id=0, vmem_limit_bytes=24 * 2**20, has_side_effects=True),
             name="window",
-        )(state)
+        )(pltpu.with_memory_space_constraint(state, pltpu.HBM))
 
     return jax.shard_map(
         body,

time: 47.1 us -> 46.3 us (0.983)
  local copies, waits for them, and re-layouts: 1.7 us -> 0.73 us
    unnamed x3 -> x1, local copies, waits for them, and re-layouts: 1.7 us -> 0.73 us
where the time goes in v2:
time: 46.3 us; the launch traced here: 46.2 us
  Pallas kernels  45.4 us (98%)
  local copies, waits for them, and re-layouts  0.73 us (2%)
    pallas_call x1, Pallas kernels, body(): pl.pallas_call(lambda *refs: kernel(nxp, nzh, *refs), out_shape=jax.Shape...  45.4 us

profile of v2, /device:TPU:24, one launch (start us, length us, event | category | flops | bytes accessed | tf_op | source)
XLA Modules:
  0.0 46.2 jit_solution(10672963411197684406)
XLA Ops:
  0.0 45.4 %window.1 = f32[1,5,8,16,128]{4,3,2,1,0:T(8,128)S(1)} custom-call(f32[5,8,16,128]{3,2,1,0:T(8,128)} %refs_0_.1), custom_call_target="tpu_custom_call" | custom-call | tf_op jit(solution)/shard_map/window/pallas_call | solution.py:330
  45.5 0.7 %copy.3 = f32[1,5,8,16,128]{4,3,2,1,0:T(8,128)} copy(f32[1,5,8,16,128]{4,3,2,1,0:T(8,128)S(1)} %window.1) | data formatting | bytes 655360

commit v3 on v2

--- a/solution.py
+++ b/solution.py
@@ -83,7 +83,7 @@
     gy = lax.axis_index("gy")
     h, c = gy // 2, gy % 2
     x, lo = gx % nxp, gx // nxp
-    q = y // 2
+    q = 1 - y // 2
     back = ((y + 1) // 2 + 1) % 2
     mine_x = back * nxp + x
     pos = q + lo * (3 - 2 * q)
@@ -94,7 +94,7 @@
         h2, pos2 = index // 4, index % 4
         lo2 = pos2 // 2
         q2 = pos2 + lo2 * (3 - 2 * pos2)
-        return (1 + q2 + (column // nxp) * (2 * q2 - 1), lo2 * nxp + column % nxp, h2 * 2 + core)
+        return (2 - q2 + (column // nxp) * (1 - 2 * q2), lo2 * nxp + column % nxp, h2 * 2 + core)
 
     yi = h * 4 + pos
     nx = 2 * nxp

time: 46.3 us -> 45.5 us (0.983)
  Pallas kernels: 45.4 us -> 44.6 us
    pallas_call x1, Pallas kernels: 45.4 us -> 44.6 us  [body(): pl.pallas_call(lambda *refs: kernel(nxp, nzh, *refs), out_shape=jax.Shape...]
where the time goes in v3:
time: 45.5 us; the launch traced here: 45.4 us
  Pallas kernels  44.6 us (98%)
  local copies, waits for them, and re-layouts  0.73 us (2%)
    pallas_call x1, Pallas kernels, body(): pl.pallas_call(lambda *refs: kernel(nxp, nzh, *refs), out_shape=jax.Shape...  44.6 us

profile of v3, /device:TPU:24, one launch (start us, length us, event | category | flops | bytes accessed | tf_op | source)
XLA Modules:
  0.0 45.4 jit_solution(4022886673785841219)
XLA Ops:
  0.0 44.6 %window.1 = f32[1,5,8,16,128]{4,3,2,1,0:T(8,128)S(1)} custom-call(f32[5,8,16,128]{3,2,1,0:T(8,128)} %refs_0_.1), custom_call_target="tpu_custom_call" | custom-call | tf_op jit(solution)/shard_map/window/pallas_call | solution.py:330
  44.6 0.7 %copy.3 = f32[1,5,8,16,128]{4,3,2,1,0:T(8,128)} copy(f32[1,5,8,16,128]{4,3,2,1,0:T(8,128)S(1)} %window.1) | data formatting | bytes 655360

commit v4 on v3

--- a/solution.py
+++ b/solution.py
@@ -166,12 +166,12 @@
         else:
             for i in range(5):
                 xe[slot, i, 4:8] = value[i]
-        for copy in along[:2]:
-            copy.start()
         for i in range(5):
             sy[slot, 0, i] = value[i][:, 0:4]
             sy[slot, 1, i] = value[i][:, 4:8]
         for copy in along[2:]:
+            copy.start()
+        for copy in along[:2]:
             copy.start()
 
     def receive(slot):
@@ -277,7 +277,6 @@
     evaluate(U12, TB2, begun[2])
     send(U22, mix(("g", TB2, 5 / 12 * DT), base=base22))
     send(U13, mix(("g", TB2, DT), base=base13))
-    finals.append(final(1, xe.at[U13, :, pl.ds(4, 4)]))
     begun = begin(U31), begin(U22), begin(U13)
     base32 = mix(("u", U31, 1.0), ("g", TC1, -4 / 12 * DT), ("g", F0, -1 / 12 * DT))
     base23 = mix(("u", U22, 1.0), ("g", TB2, -4 / 12 * DT), ("g", TB1, -1 / 12 * DT))
@@ -289,6 +288,7 @@
     send(U32, mix(("g", TC2, 5 / 12 * DT), base=base32))
     base23 = mix(("g", TC2, DT), base=base23)
     receive(U13)
+    finals.append(final(1, xe.at[U13, :, pl.ds(4, 4)]))
     evaluate(U13, TB3, begun[2])
     send(U23, mix(("g", TB3, 5 / 12 * DT), base=base23))
     finals.append(final(2, xe.at[U23, :, pl.ds(4, 4)]))

time: 45.5 us -> 45.4 us (level)
  no operation moved by 1% of the time
where the time goes in v4:
time: 45.4 us; the launch traced here: 45.2 us
  Pallas kernels  44.5 us (98%)
  local copies, waits for them, and re-layouts  0.73 us (2%)
    pallas_call x1, Pallas kernels, body(): pl.pallas_call(lambda *refs: kernel(nxp, nzh, *refs), out_shape=jax.Shape...  44.5 us

profile of v4, /device:TPU:24, one launch (start us, length us, event | category | flops | bytes accessed | tf_op | source)
XLA Modules:
  0.0 45.2 jit_solution(16358728733449811121)
XLA Ops:
  0.0 44.5 %window.1 = f32[1,5,8,16,128]{4,3,2,1,0:T(8,128)S(1)} custom-call(f32[5,8,16,128]{3,2,1,0:T(8,128)} %refs_0_.1), custom_call_target="tpu_custom_call" | custom-call | tf_op jit(solution)/shard_map/window/pallas_call | solution.py:330
  44.5 0.7 %copy.3 = f32[1,5,8,16,128]{4,3,2,1,0:T(8,128)} copy(f32[1,5,8,16,128]{4,3,2,1,0:T(8,128)S(1)} %window.1) | data formatting | bytes 655360
